TPU v7x, 32 devices: a whole 2x2x4 slice. The times are simulated.
32 devices in a mesh: groups: 2 (over y), tm: 4 (over z), batch: 2 (over x), rep: 2 (over core).
Axes of the slice: x: 2, y: 2, z: 4, core: 2. Of those that a mesh axis runs over, the one named last changes fastest.
Arguments:
- latents: bfloat16 [8, 2048, 512], P(('groups', 'batch', 'rep'), 'tm'), parts along dimension 0, may hold values from -6 to 6
- session_ids: int32 [8], P(('groups', 'batch', 'rep')), parts along dimension 0, may hold values from 0 to 7
- session_gain: float32 [8, 512], replicated, may hold values from 0.25 to 1.75
- session_shift: float32 [8, 512], replicated, may hold values from -3 to 3
- first_conv_weight: bfloat16 [3, 512, 512], replicated, may hold values from -0.15625 to 0.15625
- first_conv_bias: float32 [512], replicated, may hold values from -1.5 to 1.5
- second_conv_weight: bfloat16 [3, 512, 512], replicated, may hold values from -0.15625 to 0.15625
- second_conv_bias: float32 [512], replicated, may hold values from -1.5 to 1.5
- proj_weight: bfloat16 [512, 128], replicated, may hold values from -0.25 to 0.25
- offsets: int32 [8, 2048], P(('groups', 'batch', 'rep'), 'tm'), parts along dimension 0, may hold values from 1 to 10
- counts: int32 [8, 4], P(('groups', 'batch', 'rep'), 'tm'), parts along dimension 0, may hold values from 128 to 512, as said below
Outputs:
- embedding: bfloat16 [8, 2048, 128], P(('groups', 'batch', 'rep'), 'tm'), parts along dimension 0
- grad_conv: float32 [6, 512, 512], P('groups', None, 'tm'), parts along dimension 0
- grad_bias: float32 [1024], P(('groups', 'tm')), parts along dimension 0
- grad_proj: float32 [1024, 128], P(('groups', 'tm')), parts along dimension 0
There are 2 independent parts, one for each index of `groups`. A program takes and returns all parts, laid end to end along the dimension named above; an argument that names none is the same for every part. Nothing has to cross between parts.
Inputs may be any that keep to these rules, and one draw needn't show every extreme that they name: `counts`: bin t of a slab is live when t is below the slab's count.
All inputs are finite; a program needn't handle non-finite values.
Results may differ from a plain program's by a relative error of at most 0.0063.
Values may be sent and summed in bfloat16 or wider, within the bound.
A program may use at most 64 MiB of HBM per device.

v0:
```python
import jax
import jax.numpy as jnp
from jax import lax
from jax.sharding import PartitionSpec as P

FIRST_DILATION = 1
SECOND_DILATION = 2
OFF_MAX = 10
reciprocal_softness = 2.0


def padded_2(block, sides, width):
    for axis, dim in sides:
        count = lax.axis_size(axis)
        forward = [(i, i + 1) for i in range(count - 1)]
        backward = [(target, source) for source, target in forward]
        low = lax.ppermute(
            lax.slice_in_dim(block, block.shape[dim] - width, None, axis=dim), axis, forward
        )
        high = lax.ppermute(lax.slice_in_dim(block, 0, width, axis=dim), axis, backward)
        block = jnp.concatenate([low, block, high], axis=dim)
    return block


def passed_along(value, axis, steps):
    count = lax.axis_size(axis)
    leading, last = (max(0, -steps), min(count, count - steps))
    return lax.ppermute(value, axis, [(source, source + steps) for source in range(leading, last)])


def convolved_rows(padded, couple_coefficient, bias, dilation, count):
    total = jnp.zeros((count, couple_coefficient.shape[2]), jnp.float32) + bias[None, :]
    for filter_tap_index in range(3):
        shifted = padded[filter_tap_index * dilation : filter_tap_index * dilation + count]
        total = total + jnp.dot(
            shifted, couple_coefficient[filter_tap_index], preferred_element_type=jnp.float32
        )
    return total


def pair_weights(embed, piece_embed, portion_valid, own_first):
    cosine_affinity_matrix = reciprocal_softness * lax.dot_general(
        embed, piece_embed, (((1,), (1,)), ((), ())), preferred_element_type=jnp.float32
    )
    local_embedding = own_first + jnp.arange(embed.shape[0])[:, None]
    remote_embedding = jnp.arange(piece_embed.shape[0])[None, :]
    return (
        jnp.where(
            local_embedding != remote_embedding,
            jnp.exp(cosine_affinity_matrix - reciprocal_softness),
            0.0,
        )
        * portion_valid[None, :]
    )


def per_device(
    latents,
    session_ids,
    session_gain,
    session_shift,
    first_conv_weight,
    first_conv_bias,
    second_conv_weight,
    second_conv_bias,
    proj_weight,
    offsets,
    counts,
):
    count_of_rows = latents.shape[1]
    channels = latents.shape[2]
    slab_index = lax.axis_index("tm")
    slab_count = lax.axis_size("tm")
    picker = (session_ids[:, None] == jnp.arange(session_gain.shape[0])[None, :]).astype(
        jnp.float32
    )
    gain_row = jnp.dot(picker, session_gain, precision=lax.Precision.HIGHEST)
    shift_row = jnp.dot(picker, session_shift, precision=lax.Precision.HIGHEST)
    base_offset = (latents[0].astype(jnp.float32) * gain_row + shift_row).astype(jnp.bfloat16)
    input_padded = padded_2(base_offset, (("tm", 0),), FIRST_DILATION)
    first_preactivation = convolved_rows(
        input_padded, first_conv_weight, first_conv_bias, FIRST_DILATION, count_of_rows
    )
    first_hidden = (base_offset.astype(jnp.float32) + jax.nn.gelu(first_preactivation)).astype(
        jnp.bfloat16
    )
    first_padded = padded_2(first_hidden, (("tm", 0),), SECOND_DILATION)
    second_preactivation = convolved_rows(
        first_padded, second_conv_weight, second_conv_bias, SECOND_DILATION, count_of_rows
    )
    hidden_two = (first_hidden.astype(jnp.float32) + jax.nn.gelu(second_preactivation)).astype(
        jnp.bfloat16
    )
    feats = jnp.dot(hidden_two, proj_weight, preferred_element_type=jnp.float32)
    scale = lax.rsqrt(jnp.sum(feats * feats, axis=1) + 1e-06)
    unit = feats * scale[:, None]
    embed = unit.astype(jnp.bfloat16)
    usable_mask_vector = (jnp.arange(count_of_rows) < counts[0, 0]).astype(jnp.float32)
    live_flags = usable_mask_vector.astype(jnp.bfloat16)
    earlier = passed_along(embed[count_of_rows - OFF_MAX :], "tm", 1)
    extended = jnp.concatenate([earlier, embed], axis=0)
    slab_first = slab_index * count_of_rows
    moment = slab_first + jnp.arange(count_of_rows)
    back_time = moment - offsets[0]
    target = jnp.where(back_time >= 0, back_time, moment + offsets[0])
    local_index = target - slab_first + OFF_MAX
    matched_sample_vector = extended[local_index].astype(jnp.float32)
    own_first = lax.axis_index("batch") * count_of_rows
    piece_embed = lax.all_gather(embed, "batch", axis=0, tiled=True)
    portion_valid = lax.all_gather(live_flags, "batch", axis=0, tiled=True)
    couple_coefficient = pair_weights(
        embed, piece_embed, portion_valid.astype(jnp.float32), own_first
    )
    denom = jnp.sum(couple_coefficient, axis=1)
    piece_embed = lax.all_gather(embed.astype(jnp.float32), "batch", axis=0, tiled=True)
    portion_valid = lax.all_gather(usable_mask_vector, "batch", axis=0, tiled=True)
    piece_denom = lax.all_gather(denom, "batch", axis=0, tiled=True)
    add_piece_embed = piece_embed.astype(jnp.bfloat16)
    couple_coefficient = pair_weights(embed, add_piece_embed, portion_valid, own_first)
    soft = (couple_coefficient / denom[:, None]).astype(jnp.bfloat16)
    reverse = (couple_coefficient * usable_mask_vector[:, None] / piece_denom[None, :]).astype(
        jnp.bfloat16
    )
    anchor_sum = jnp.dot(soft, add_piece_embed, preferred_element_type=jnp.float32)
    pooled_sum = jnp.dot(reverse, add_piece_embed, preferred_element_type=jnp.float32)
    anchor_sum, pooled_sum = (anchor_sum, pooled_sum)
    propagated_samples = (
        jnp.zeros((OFF_MAX + count_of_rows, embed.shape[1]), jnp.float32)
        .at[local_index]
        .add(usable_mask_vector[:, None] * embed.astype(jnp.float32))
    )
    returned = passed_along(propagated_samples[:OFF_MAX], "tm", -1)
    pushed_own = propagated_samples[OFF_MAX:].at[count_of_rows - OFF_MAX :].add(returned)
    unit_length_derivative = reciprocal_softness * (
        usable_mask_vector[:, None] * (anchor_sum - matched_sample_vector) + pooled_sum - pushed_own
    )
    along = jnp.sum(unit * unit_length_derivative, axis=1, keepdims=True)
    grad_feat = ((unit_length_derivative - unit * along) * scale[:, None]).astype(jnp.bfloat16)
    grad_proj = lax.dot_general(
        hidden_two, grad_feat, (((0,), (0,)), ((), ())), preferred_element_type=jnp.float32
    )
    grad_hidden = lax.dot_general(
        grad_feat, proj_weight, (((1,), (1,)), ((), ())), preferred_element_type=jnp.float32
    )
    unused, pull = jax.vjp(jax.nn.gelu, second_preactivation)
    gradient_preactivation = pull(grad_hidden)[0].astype(jnp.bfloat16)
    grad_bias = jnp.sum(gradient_preactivation.astype(jnp.float32), axis=0)
    grad_conv = jnp.stack(
        [
            lax.dot_general(
                first_padded[
                    filter_tap_index * SECOND_DILATION : filter_tap_index * SECOND_DILATION
                    + count_of_rows
                ],
                gradient_preactivation,
                (((0,), (0,)), ((), ())),
                preferred_element_type=jnp.float32,
            )
            for filter_tap_index in range(3)
        ]
    )
    share = channels // slab_count
    conv_total, bias_total, proj_total = lax.psum(
        (grad_conv, grad_bias, grad_proj), ("tm", "batch", "rep")
    )
    conv_part = lax.dynamic_slice_in_dim(conv_total, slab_index * share, share, 2)
    bias_part = lax.dynamic_slice_in_dim(bias_total, slab_index * share, share, 0)
    proj_part = lax.dynamic_slice_in_dim(proj_total, slab_index * share, share, 0)
    return (embed[None], conv_part, bias_part, proj_part)


def solution(mesh):
    return jax.shard_map(
        per_device,
        mesh=mesh,
        in_specs=(
            P(("groups", "batch", "rep"), "tm", None),
            P(("groups", "batch", "rep")),
            P(),
            P(),
            P(),
            P(),
            P(),
            P(),
            P(),
            P(("groups", "batch", "rep"), "tm"),
            P(("groups", "batch", "rep"), "tm"),
        ),
        out_specs=(
            P(("groups", "batch", "rep"), "tm", None),
            P("groups", None, "tm"),
            P(("groups", "tm")),
            P(("groups", "tm"), None),
        ),
        check_vma=False,
    )
```

profile of v0, /device:TPU:0, one launch (start us, length us, event | category | flops | bytes accessed | tf_op | source)
XLA Modules:
  0.0 196.3 jit_solution(15781710611473754294)
XLA Ops:
  8.0 0.8 fusion.55
  8.9 0.8 fusion.53
  9.7 1.2 fusion.6
  10.9 1.3 collective-permute-start.1
  12.2 5.6 %collective-permute-start = (bf16[1,512]{1,0:T(2,128)(2,1)S(1)}, bf16[1,512]{1,0:T(2,128)(2,1)S(1)}, u32[]{:S(2)}, u32[]{:S(2)}) collective-permute-start(bf16[1,512]{1,0:T(2,128)(2,1)S(1)} %get-tuple-element.21), channel_id=1, source_target_pairs={{0,4},{4,8},{8,12},{1,5},{5,9},{9,13},{2,6},{6,10},{10,14},{3,7},{... | collective-permute-start | bytes 3080 | tf_op jit(solution)/shard_map/ppermute | solution.py:17
  18.5 4.3 %all-gather.1 = bf16[2,1,512]{2,1,0:T(2,128)(2,1)S(1)} all-gather(bf16[1,1,512]{2,1,0:T(2,128)(2,1)S(1)} %reshape.147), channel_id=1, replica_groups=mesh['groups'=2,'tm'=4,'batch'=2,'rep'=2] {'batch'}, dimensions={0}, use_global_device_ids=true | all-gather | bytes 3072 | tf_op jit(solution)/shard_map/all_gather | solution.py:110
  23.5 1.6 fusion.27
  25.2 4.3 %all-gather = f32[2,1,512]{2,1,0:T(1,128)S(1)} all-gather(f32[1,1,512]{2,1,0:T(1,128)S(1)} %bitcast.87), channel_id=1, replica_groups=mesh['groups'=2,'tm'=4,'batch'=2,'rep'=2] {'batch'}, dimensions={0}, use_global_device_ids=true | all-gather | bytes 6144 | tf_op jit(solution)/shard_map/all_gather | solution.py:116
  30.0 0.8 fusion.24
  30.8 1.3 collective-permute-start.3
  32.1 4.5 %collective-permute-start.2 = (bf16[2,512]{1,0:T(2,128)(2,1)S(1)}, bf16[2,512]{1,0:T(2,128)(2,1)S(1)}, u32[]{:S(2)}, u32[]{:S(2)}) collective-permute-start(bf16[2,512]{1,0:T(2,128)(2,1)S(1)} %get-tuple-element.19), channel_id=1, source_target_pairs={{0,4},{4,8},{8,12},{1,5},{5,9},{9,13},{2,6},{6,10},{10,14},{3,7},{... | collective-permute-start | bytes 6152 | tf_op jit(solution)/shard_map/ppermute | solution.py:17
  37.1 0.8 collective-permute-done.2
  38.4 1.7 add_convert_fusion
  40.7 6.7 %all_gather.15 = bf16[1024,128]{1,0:T(8,128)(2,1)S(1)} all-gather(bf16[512,128]{1,0:T(8,128)(2,1)S(1)} %multiply_convert_fusion.1), channel_id=1, replica_groups=mesh['groups'=2,'tm'=4,'batch'=2,'rep'=2] {'batch'}, dimensions={0}, use_global_device_ids=true | all-gather | bytes 393216 | tf_op jit(solution)/shard_map/all_gather | solution.py:115
  47.4 5.6 %all_gather.17 = bf16[1024,128]{1,0:T(8,128)(2,1)S(1)} all-gather(bf16[512,128]{1,0:T(8,128)(2,1)S(1)} %multiply_convert_fusion.1), channel_id=1, replica_groups=mesh['groups'=2,'tm'=4,'batch'=2,'rep'=2] {'batch'}, dimensions={0}, use_global_device_ids=true | all-gather | bytes 393216 | tf_op jit(solution)/shard_map/all_gather | solution.py:109
  53.0 3.9 %collective-permute-start.4 = (bf16[10,128]{1,0:T(8,128)(2,1)S(1)}, bf16[10,128]{1,0:T(8,128)(2,1)S(1)}, u32[]{:S(2)}, u32[]{:S(2)}) collective-permute-start(bf16[10,128]{1,0:T(8,128)(2,1)S(1)} %slice.101), channel_id=1, source_target_pairs={{0,4},{4,8},{8,12},{1,5},{5,9},{9,13},{2,6},{6,10},{10,14},{3,7},{... | collective-permute-start | bytes 7688 | tf_op jit(solution)/shard_map/ppermute | solution.py:28
  56.9 2.5 %scatter_custom_fusion = f32[522,128]{1,0:T(8,128)S(1)} fusion(s32[512]{0:T(512)S(1)} %bitcast.93, f32[]{:T(128)} %constant.57.clone.1, f32[512]{0:T(512)S(1)} %fusion.52, f32[512,128]{1,0:T(8,128)S(1)} %get-tuple-element.25, f32[512]{0:T(512)S(1)} %add_rsqrt_fusion), kind=kCustom, calls=%fused_computation.74 | custom fusion | flops 327680 | bytes 533508 | tf_op jit(solution)/shard_map/scatter-add | solution.py:130
  59.4 1.3 collective-permute-start.5
  60.7 0.9 multiply_reduce_fusion
  61.5 0.7 select_multiply_fusion
  62.8 0.8 copy-done.6
  63.6 4.3 %all-gather.2 = f32[2,1,512]{2,1,0:T(1,128)S(1)} all-gather(f32[1,1,512]{2,1,0:T(1,128)S(1)} %bitcast.97), channel_id=1, replica_groups=mesh['groups'=2,'tm'=4,'batch'=2,'rep'=2] {'batch'}, dimensions={0}, use_global_device_ids=true | all-gather | bytes 6144 | tf_op jit(solution)/shard_map/all_gather | solution.py:117
  68.0 1.3 gather_fusion
  69.6 2.3 %multiply_reduce_fusion.1 = (f32[512]{0:T(512)S(1)}, f32[512,128]{1,0:T(8,128)S(1)}) fusion(f32[512,128]{1,0:T(8,128)S(1)} %get-tuple-element.25, f32[512]{0:T(512)S(1)} %add_rsqrt_fusion, f32[512,128]{1,0:T(8,128)S(1)} %scatter-add.13, bf16[1024,128]{1,0:T(8,128)(2,1)S(1)} %all_gather.15, f32[512,1024]{1,0:T(8,128)} %copy-done.6, f32[1024]{0:T(1024)S(1)} %bitcast.95, ...), kind=kOutput, calls=%fused_computation.73 | convolution fusion | flops 136379904 | bytes 3549184 | tf_op jit(solution)/shard_map/dot_general | solution.py:125
  72.1 1.0 fusion.75
  73.1 0.9 convert_reduce_fusion
  75.4 2.0 %pad_maximum_fusion = f32[3,512,512]{2,1,0:T(8,128)} fusion(f32[1,512,512]{2,1,0:T(8,128)S(1)} %convolution_bitcast_fusion, f32[1,512,512]{2,1,0:T(8,128)S(1)} %convolution_bitcast_fusion.1, f32[1,512,512]{2,1,0:T(8,128)S(1)} %convolution_bitcast_fusion.2), kind=kLoop, calls=%fused_computation.2 | loop fusion | flops 1572864 | bytes 6291456 | tf_op jit(solution)/shard_map/stack | solution.py:148
  77.4 0.8 fusion.95
  78.2 31.1 %psum.22 = f32[512]{0:T(512)S(1)} all-reduce(f32[512]{0:T(512)S(1)} %get-tuple-element.28), channel_id=1, replica_groups=mesh['groups'=2,'tm'=4,'batch'=2,'rep'=2] {'tm','batch','rep'}, use_global_device_ids=true, to_apply=%region_6.7 | all-reduce | flops 512 | bytes 4096 | tf_op jit(solution)/shard_map/psum | solution.py:163
  109.9 76.0 %all-reduce.3.cloned.1.call-done = (f32[3,512,512]{2,1,0:T(8,128)}, f32[512,128]{1,0:T(8,128)}) async-done(((f32[3,512,512]{2,1,0:T(8,128)}, f32[512,128]{1,0:T(8,128)}), (f32[3,512,512]{2,1,0:T(8,128)}, f32[512,128]{1,0:T(8,128)})) %all-reduce.3.cloned.1.call-update) | async-done | bytes 3407888 | tf_op jit(solution)/shard_map/psum | solution.py:163
  185.9 2.1 %constant_dynamic-slice_fusion.1 = f32[3,512,128]{2,1,0:T(8,128)} fusion(f32[3,512,512]{2,1,0:T(8,128)} %get-tuple-element.16, s32[]{:T(128)S(6)} %select_n.38), kind=kLoop, calls=%fused_computation.103 | loop fusion | bytes 1572868 | tf_op jit(solution)/shard_map/dynamic_slice | solution.py:166
  188.0 1.5 constant_dynamic-slice_fusion
  (47 shorter events, 5.6 us)
Async XLA Ops:
  7.2 33.0 %copy-start = (bf16[512,128]{1,0:T(8,128)(2,1)S(1)}, bf16[512,128]{1,0:T(8,128)(2,1)}, u32[]{:S(2)}) copy-start(bf16[512,128]{1,0:T(8,128)(2,1)} %param.21) | copy-start | bytes 393220
  7.2 22.3 %copy-start.2 = (bf16[3,512,512]{2,1,0:T(8,128)(2,1)S(1)}, bf16[3,512,512]{2,1,0:T(8,128)(2,1)}, u32[]{:S(2)}) copy-start(bf16[3,512,512]{2,1,0:T(8,128)(2,1)} %param.17) | copy-start | bytes 4718596
  7.2 22.3 %copy-start.3 = (f32[512]{0:T(512)S(1)}, f32[512]{0:T(512)}, u32[]{:S(2)}) copy-start(f32[512]{0:T(512)} %param.18) | copy-start | bytes 6148
  7.2 178.7 %all-reduce.3.cloned.1.call-start = ((), (), s32[]{:S(2)}) async-start(), calls=%async_computation | async-start | bytes 6815744 | tf_op jit(solution)/shard_map/psum | solution.py:163
  10.9 19.1 %collective-permute-start.1 = (bf16[1,512]{1,0:T(2,128)(2,1)S(1)}, bf16[1,512]{1,0:T(2,128)(2,1)S(1)}, u32[]{:S(2)}, u32[]{:S(2)}) collective-permute-start(bf16[1,512]{1,0:T(2,128)(2,1)S(1)} %get-tuple-element.20), channel_id=1, source_target_pairs={{4,0},{8,4},{12,8},{5,1},{9,5},{13,9},{6,2},{10,6},{14,10},{7,3},{... | collective-permute-start | bytes 3080 | tf_op jit(solution)/shard_map/ppermute | solution.py:20
  12.2 17.3 %collective-permute-start = (bf16[1,512]{1,0:T(2,128)(2,1)S(1)}, bf16[1,512]{1,0:T(2,128)(2,1)S(1)}, u32[]{:S(2)}, u32[]{:S(2)}) collective-permute-start(bf16[1,512]{1,0:T(2,128)(2,1)S(1)} %get-tuple-element.21), channel_id=1, source_target_pairs={{0,4},{4,8},{8,12},{1,5},{5,9},{9,13},{2,6},{6,10},{10,14},{3,7},{... | collective-permute-start | bytes 3080 | tf_op jit(solution)/shard_map/ppermute | solution.py:17
  30.0 6.7 %copy-start.1 = (bf16[3,512,512]{2,1,0:T(8,128)(2,1)S(1)}, bf16[3,512,512]{2,1,0:T(8,128)(2,1)}, u32[]{:S(2)}) copy-start(bf16[3,512,512]{2,1,0:T(8,128)(2,1)} %param.19) | copy-start | bytes 4718596
  30.8 7.2 %copy-start.4 = (f32[512]{0:T(512)S(1)}, f32[512]{0:T(512)}, u32[]{:S(2)}) copy-start(f32[512]{0:T(512)} %param.20) | copy-start | bytes 6148
  30.8 7.6 %collective-permute-start.3 = (bf16[2,512]{1,0:T(2,128)(2,1)S(1)}, bf16[2,512]{1,0:T(2,128)(2,1)S(1)}, u32[]{:S(2)}, u32[]{:S(2)}) collective-permute-start(bf16[2,512]{1,0:T(2,128)(2,1)S(1)} %get-tuple-element.18), channel_id=1, source_target_pairs={{4,0},{8,4},{12,8},{5,1},{9,5},{13,9},{6,2},{10,6},{14,10},{7,3},{... | collective-permute-start | bytes 6152 | tf_op jit(solution)/shard_map/ppermute | solution.py:20
  32.1 5.8 %collective-permute-start.2 = (bf16[2,512]{1,0:T(2,128)(2,1)S(1)}, bf16[2,512]{1,0:T(2,128)(2,1)S(1)}, u32[]{:S(2)}, u32[]{:S(2)}) collective-permute-start(bf16[2,512]{1,0:T(2,128)(2,1)S(1)} %get-tuple-element.19), channel_id=1, source_target_pairs={{0,4},{4,8},{8,12},{1,5},{5,9},{9,13},{2,6},{6,10},{10,14},{3,7},{... | collective-permute-start | bytes 6152 | tf_op jit(solution)/shard_map/ppermute | solution.py:17
  53.0 15.0 %collective-permute-start.4 = (bf16[10,128]{1,0:T(8,128)(2,1)S(1)}, bf16[10,128]{1,0:T(8,128)(2,1)S(1)}, u32[]{:S(2)}, u32[]{:S(2)}) collective-permute-start(bf16[10,128]{1,0:T(8,128)(2,1)S(1)} %slice.101), channel_id=1, source_target_pairs={{0,4},{4,8},{8,12},{1,5},{5,9},{9,13},{2,6},{6,10},{10,14},{3,7},{... | collective-permute-start | bytes 7688 | tf_op jit(solution)/shard_map/ppermute | solution.py:28
  59.4 10.0 %collective-permute-start.5 = (f32[10,128]{1,0:T(8,128)S(1)}, f32[10,128]{1,0:T(8,128)S(1)}, u32[]{:S(2)}, u32[]{:S(2)}) collective-permute-start(f32[10,128]{1,0:T(8,128)S(1)} %slice.104), channel_id=1, source_target_pairs={{4,0},{8,4},{12,8},{5,1},{9,5},{13,9},{6,2},{10,6},{14,10},{7,3},{... | collective-permute-start | bytes 15368 | tf_op jit(solution)/shard_map/ppermute | solution.py:28
  62.3 1.3 copy-start.6
  69.5 3.6 %copy-start.5 = (f32[512,512]{1,0:T(8,128)S(1)}, f32[512,512]{1,0:T(8,128)}, u32[]{:S(2)}) copy-start(f32[512,512]{1,0:T(8,128)} %get-tuple-element.23) | copy-start | bytes 3145732
Sparse Core Ops, SparseCore 0:
  77.5 108.3 all-reduce.2
where the time goes:
time: 197 us; the launch traced here: 196 us
  waiting for transfers between devices  76.9 us (39%)
  blocking collectives  56.4 us (29%)
  starting transfers between devices  17.9 us (9%)
  between operations  15.8 us (8%)
  matrix products  15.2 us (8%)
  other arithmetic  7.54 us (4%)
  local copies, waits for them, and re-layouts  6.55 us (3%)
    psum x1, waiting for transfers between devices, per_device(): lax.psum((grad_conv, grad_bias, grad_proj), ('tm', 'batch', 'rep'))  76 us
    psum x1, blocking collectives, per_device(): lax.psum((grad_conv, grad_bias, grad_proj), ('tm', 'batch', 'rep'))  31.1 us
    ppermute x2, starting transfers between devices, padded_2(): lax.ppermute(lax.slice_in_dim(block, block.shape[dim] - width, None, axis...  10.1 us
    all_gather x1, blocking collectives, per_device(): lax.all_gather(embed.astype(jnp.float32), 'batch', axis=0, tiled=True)  6.66 us
    all_gather x1, blocking collectives, per_device(): piece_embed = lax.all_gather(embed, 'batch', axis=0, tiled=True)  5.63 us
    dot_general x6, matrix products, convolved_rows(): jnp.dot(shifted, couple_coefficient[filter_tap_index], preferred_element_...  5.48 us
    ppermute x2, starting transfers between devices, passed_along(): lax.ppermute(value, axis, [(source, source + steps) for source in range(l...  5.17 us
    all_gather x1, blocking collectives, per_device(): lax.all_gather(usable_mask_vector, 'batch', axis=0, tiled=True)  4.34 us
  transfers between devices with their start and end apart: 7, of which 2 were waited for; matrix products, arithmetic and copies ran while one was open for 6% of the time, Pallas kernels for 0%

commit v1 on v0

--- a/solution.py
+++ b/solution.py
@@ -161,7 +161,7 @@
     )
     share = channels // slab_count
     conv_total, bias_total, proj_total = lax.psum(
-        (grad_conv, grad_bias, grad_proj), ("tm", "batch", "rep")
+        lax.psum((grad_conv, grad_bias, grad_proj), ("batch", "rep")), "tm"
     )
     conv_part = lax.dynamic_slice_in_dim(conv_total, slab_index * share, share, 2)
     bias_part = lax.dynamic_slice_in_dim(bias_total, slab_index * share, share, 0)

time: 197 us -> 297 us (1.51)
  waiting for transfers between devices: 76.9 us -> 189 us
  blocking collectives: 56.4 us -> 43.4 us
    psum x1 -> x2, waiting for transfers between devices: 76 us -> 189 us  [the longest x1 113 us: per_device(): lax.psum(lax.psum((grad_conv, grad_bias, grad_proj), ('batch', 'rep')), '...]
    psum x1 -> x2, blocking collectives: 31.1 us -> 18.1 us  [the longest x1 12.3 us: per_device(): lax.psum(lax.psum((grad_conv, grad_bias, grad_proj), ('batch', 'rep')), '...]
  transfers between devices with their start and end apart: 7 -> 8, of which waited for: 2 -> 3; matrix products, arithmetic and copies ran while one was open for 6% -> 4% of each run, Pallas kernels for 0% -> 0%
where the time goes in v1:
time: 297 us; the launch traced here: 296 us
  waiting for transfers between devices  189 us (64%)
  blocking collectives  43.4 us (15%)
  starting transfers between devices  17.9 us (6%)
  between operations  15.8 us (5%)
  matrix products  15.2 us (5%)
  other arithmetic  7.55 us (3%)
  local copies, waits for them, and re-layouts  6.55 us (2%)
    psum x1, waiting for transfers between devices, per_device(): lax.psum(lax.psum((grad_conv, grad_bias, grad_proj), ('batch', 'rep')), '...  113 us
    psum x1, waiting for transfers between devices, per_device(): lax.psum((grad_conv, grad_bias, grad_proj), ('batch', 'rep'))  75.4 us
    psum x1, blocking collectives, per_device(): lax.psum(lax.psum((grad_conv, grad_bias, grad_proj), ('batch', 'rep')), '...  12.3 us
    ppermute x2, starting transfers between devices, padded_2(): lax.ppermute(lax.slice_in_dim(block, block.shape[dim] - width, None, axis...  10.1 us
    all_gather x1, blocking collectives, per_device(): lax.all_gather(embed.astype(jnp.float32), 'batch', axis=0, tiled=True)  6.66 us
  transfers between devices with their start and end apart: 8, of which 3 were waited for; matrix products, arithmetic and copies ran while one was open for 4% of the time, Pallas kernels for 0%

profile of v1, /device:TPU:0, one launch (start us, length us, event | category | flops | bytes accessed | tf_op | source)
XLA Modules:
  0.0 295.9 jit_solution(2540276817413431687)
XLA Ops:
  8.0 0.8 fusion.55
  8.9 0.8 fusion.53
  9.7 1.2 fusion.6
  10.9 1.3 collective-permute-start.1
  12.2 5.6 %collective-permute-start = (bf16[1,512]{1,0:T(2,128)(2,1)S(1)}, bf16[1,512]{1,0:T(2,128)(2,1)S(1)}, u32[]{:S(2)}, u32[]{:S(2)}) collective-permute-start(bf16[1,512]{1,0:T(2,128)(2,1)S(1)} %get-tuple-element.23), channel_id=1, source_target_pairs={{0,4},{4,8},{8,12},{1,5},{5,9},{9,13},{2,6},{6,10},{10,14},{3,7},{... | collective-permute-start | bytes 3080 | tf_op jit(solution)/shard_map/ppermute | solution.py:17
  18.5 4.3 %all-gather.1 = bf16[2,1,512]{2,1,0:T(2,128)(2,1)S(1)} all-gather(bf16[1,1,512]{2,1,0:T(2,128)(2,1)S(1)} %reshape.147), channel_id=1, replica_groups=mesh['groups'=2,'tm'=4,'batch'=2,'rep'=2] {'batch'}, dimensions={0}, use_global_device_ids=true | all-gather | bytes 3072 | tf_op jit(solution)/shard_map/all_gather | solution.py:110
  23.5 1.6 fusion.27
  25.2 4.3 %all-gather = f32[2,1,512]{2,1,0:T(1,128)S(1)} all-gather(f32[1,1,512]{2,1,0:T(1,128)S(1)} %bitcast.87), channel_id=1, replica_groups=mesh['groups'=2,'tm'=4,'batch'=2,'rep'=2] {'batch'}, dimensions={0}, use_global_device_ids=true | all-gather | bytes 6144 | tf_op jit(solution)/shard_map/all_gather | solution.py:116
  30.8 1.3 collective-permute-start.3
  32.1 4.5 %collective-permute-start.2 = (bf16[2,512]{1,0:T(2,128)(2,1)S(1)}, bf16[2,512]{1,0:T(2,128)(2,1)S(1)}, u32[]{:S(2)}, u32[]{:S(2)}) collective-permute-start(bf16[2,512]{1,0:T(2,128)(2,1)S(1)} %get-tuple-element.21), channel_id=1, source_target_pairs={{0,4},{4,8},{8,12},{1,5},{5,9},{9,13},{2,6},{6,10},{10,14},{3,7},{... | collective-permute-start | bytes 6152 | tf_op jit(solution)/shard_map/ppermute | solution.py:17
  37.1 0.8 collective-permute-done.2
  38.4 1.7 add_convert_fusion
  40.7 6.7 %all_gather.15 = bf16[1024,128]{1,0:T(8,128)(2,1)S(1)} all-gather(bf16[512,128]{1,0:T(8,128)(2,1)S(1)} %multiply_convert_fusion.1), channel_id=1, replica_groups=mesh['groups'=2,'tm'=4,'batch'=2,'rep'=2] {'batch'}, dimensions={0}, use_global_device_ids=true | all-gather | bytes 393216 | tf_op jit(solution)/shard_map/all_gather | solution.py:115
  47.4 5.6 %all_gather.17 = bf16[1024,128]{1,0:T(8,128)(2,1)S(1)} all-gather(bf16[512,128]{1,0:T(8,128)(2,1)S(1)} %multiply_convert_fusion.1), channel_id=1, replica_groups=mesh['groups'=2,'tm'=4,'batch'=2,'rep'=2] {'batch'}, dimensions={0}, use_global_device_ids=true | all-gather | bytes 393216 | tf_op jit(solution)/shard_map/all_gather | solution.py:109
  53.0 3.9 %collective-permute-start.4 = (bf16[10,128]{1,0:T(8,128)(2,1)S(1)}, bf16[10,128]{1,0:T(8,128)(2,1)S(1)}, u32[]{:S(2)}, u32[]{:S(2)}) collective-permute-start(bf16[10,128]{1,0:T(8,128)(2,1)S(1)} %slice.101), channel_id=1, source_target_pairs={{0,4},{4,8},{8,12},{1,5},{5,9},{9,13},{2,6},{6,10},{10,14},{3,7},{... | collective-permute-start | bytes 7688 | tf_op jit(solution)/shard_map/ppermute | solution.py:28
  56.9 2.5 scatter_custom_fusion
  59.4 1.3 collective-permute-start.5
  60.7 0.9 multiply_reduce_fusion
  62.8 0.8 copy-done.6
  63.6 4.3 %all-gather.2 = f32[2,1,512]{2,1,0:T(1,128)S(1)} all-gather(f32[1,1,512]{2,1,0:T(1,128)S(1)} %bitcast.97), channel_id=1, replica_groups=mesh['groups'=2,'tm'=4,'batch'=2,'rep'=2] {'batch'}, dimensions={0}, use_global_device_ids=true | all-gather | bytes 6144 | tf_op jit(solution)/shard_map/all_gather | solution.py:117
  68.0 1.3 gather_fusion
  69.6 2.3 multiply_reduce_fusion.1
  72.1 1.0 fusion.75
  73.1 0.9 convert_reduce_fusion
  75.4 2.0 pad_maximum_fusion
  77.5 75.4 %all-reduce.5.cloned.1.call-done = (f32[3,512,512]{2,1,0:T(8,128)}, f32[512,128]{1,0:T(8,128)}) async-done(((f32[3,512,512]{2,1,0:T(8,128)}, f32[512,128]{1,0:T(8,128)}), (f32[3,512,512]{2,1,0:T(8,128)}, f32[512,128]{1,0:T(8,128)})) %all-reduce.5.cloned.1.call-update) | async-done | bytes 3407888 | tf_op jit(solution)/shard_map/psum | solution.py:164
  152.9 0.8 fusion.95
  153.7 5.8 %psum.44 = f32[512]{0:T(512)S(1)} all-reduce(f32[512]{0:T(512)S(1)} %get-tuple-element.30), channel_id=1, replica_groups=mesh['groups'=2,'tm'=4,'batch'=2,'rep'=2] {'batch','rep'}, use_global_device_ids=true, to_apply=%region_7.8 | all-reduce | flops 512 | bytes 4096 | tf_op jit(solution)/shard_map/psum | solution.py:164
  159.5 12.3 %psum.45 = f32[512]{0:T(512)S(1)} all-reduce(f32[512]{0:T(512)S(1)} %psum.44), channel_id=1, replica_groups=mesh['groups'=2,'tm'=4,'batch'=2,'rep'=2] {'tm'}, use_global_device_ids=true, to_apply=%region_8.9 | all-reduce | flops 512 | bytes 4096 | tf_op jit(solution)/shard_map/psum | solution.py:163
  172.4 113.2 %all-reduce.7.cloned.1.call-done = (f32[3,512,512]{2,1,0:T(8,128)}, f32[512,128]{1,0:T(8,128)}) async-done(((f32[3,512,512]{2,1,0:T(8,128)}, f32[512,128]{1,0:T(8,128)}), (f32[3,512,512]{2,1,0:T(8,128)}, f32[512,128]{1,0:T(8,128)})) %all-reduce.7.cloned.1.call-update) | async-done | bytes 3407888 | tf_op jit(solution)/shard_map/psum | solution.py:163
  285.5 2.1 constant_dynamic-slice_fusion.1
  287.6 1.5 constant_dynamic-slice_fusion
  (51 shorter events, 7.2 us)
Async XLA Ops:
  7.2 33.0 %copy-start = (bf16[512,128]{1,0:T(8,128)(2,1)S(1)}, bf16[512,128]{1,0:T(8,128)(2,1)}, u32[]{:S(2)}) copy-start(bf16[512,128]{1,0:T(8,128)(2,1)} %param.21) | copy-start | bytes 393220
  7.2 22.3 %copy-start.2 = (bf16[3,512,512]{2,1,0:T(8,128)(2,1)S(1)}, bf16[3,512,512]{2,1,0:T(8,128)(2,1)}, u32[]{:S(2)}) copy-start(bf16[3,512,512]{2,1,0:T(8,128)(2,1)} %param.17) | copy-start | bytes 4718596
  7.2 22.3 %copy-start.3 = (f32[512]{0:T(512)S(1)}, f32[512]{0:T(512)}, u32[]{:S(2)}) copy-start(f32[512]{0:T(512)} %param.18) | copy-start | bytes 6148
  7.2 145.7 %all-reduce.5.cloned.1.call-start = ((), (), s32[]{:S(2)}) async-start(), calls=%async_computation | async-start | bytes 6815744 | tf_op jit(solution)/shard_map/psum | solution.py:164
  10.9 19.1 %collective-permute-start.1 = (bf16[1,512]{1,0:T(2,128)(2,1)S(1)}, bf16[1,512]{1,0:T(2,128)(2,1)S(1)}, u32[]{:S(2)}, u32[]{:S(2)}) collective-permute-start(bf16[1,512]{1,0:T(2,128)(2,1)S(1)} %get-tuple-element.22), channel_id=1, source_target_pairs={{4,0},{8,4},{12,8},{5,1},{9,5},{13,9},{6,2},{10,6},{14,10},{7,3},{... | collective-permute-start | bytes 3080 | tf_op jit(solution)/shard_map/ppermute | solution.py:20
  12.2 17.3 %collective-permute-start = (bf16[1,512]{1,0:T(2,128)(2,1)S(1)}, bf16[1,512]{1,0:T(2,128)(2,1)S(1)}, u32[]{:S(2)}, u32[]{:S(2)}) collective-permute-start(bf16[1,512]{1,0:T(2,128)(2,1)S(1)} %get-tuple-element.23), channel_id=1, source_target_pairs={{0,4},{4,8},{8,12},{1,5},{5,9},{9,13},{2,6},{6,10},{10,14},{3,7},{... | collective-permute-start | bytes 3080 | tf_op jit(solution)/shard_map/ppermute | solution.py:17
  30.0 6.7 %copy-start.1 = (bf16[3,512,512]{2,1,0:T(8,128)(2,1)S(1)}, bf16[3,512,512]{2,1,0:T(8,128)(2,1)}, u32[]{:S(2)}) copy-start(bf16[3,512,512]{2,1,0:T(8,128)(2,1)} %param.19) | copy-start | bytes 4718596
  30.8 7.2 %copy-start.4 = (f32[512]{0:T(512)S(1)}, f32[512]{0:T(512)}, u32[]{:S(2)}) copy-start(f32[512]{0:T(512)} %param.20) | copy-start | bytes 6148
  30.8 7.6 %collective-permute-start.3 = (bf16[2,512]{1,0:T(2,128)(2,1)S(1)}, bf16[2,512]{1,0:T(2,128)(2,1)S(1)}, u32[]{:S(2)}, u32[]{:S(2)}) collective-permute-start(bf16[2,512]{1,0:T(2,128)(2,1)S(1)} %get-tuple-element.20), channel_id=1, source_target_pairs={{4,0},{8,4},{12,8},{5,1},{9,5},{13,9},{6,2},{10,6},{14,10},{7,3},{... | collective-permute-start | bytes 6152 | tf_op jit(solution)/shard_map/ppermute | solution.py:20
  32.1 5.8 %collective-permute-start.2 = (bf16[2,512]{1,0:T(2,128)(2,1)S(1)}, bf16[2,512]{1,0:T(2,128)(2,1)S(1)}, u32[]{:S(2)}, u32[]{:S(2)}) collective-permute-start(bf16[2,512]{1,0:T(2,128)(2,1)S(1)} %get-tuple-element.21), channel_id=1, source_target_pairs={{0,4},{4,8},{8,12},{1,5},{5,9},{9,13},{2,6},{6,10},{10,14},{3,7},{... | collective-permute-start | bytes 6152 | tf_op jit(solution)/shard_map/ppermute | solution.py:17
  53.0 15.0 %collective-permute-start.4 = (bf16[10,128]{1,0:T(8,128)(2,1)S(1)}, bf16[10,128]{1,0:T(8,128)(2,1)S(1)}, u32[]{:S(2)}, u32[]{:S(2)}) collective-permute-start(bf16[10,128]{1,0:T(8,128)(2,1)S(1)} %slice.101), channel_id=1, source_target_pairs={{0,4},{4,8},{8,12},{1,5},{5,9},{9,13},{2,6},{6,10},{10,14},{3,7},{... | collective-permute-start | bytes 7688 | tf_op jit(solution)/shard_map/ppermute | solution.py:28
  59.4 10.0 %collective-permute-start.5 = (f32[10,128]{1,0:T(8,128)S(1)}, f32[10,128]{1,0:T(8,128)S(1)}, u32[]{:S(2)}, u32[]{:S(2)}) collective-permute-start(f32[10,128]{1,0:T(8,128)S(1)} %slice.104), channel_id=1, source_target_pairs={{4,0},{8,4},{12,8},{5,1},{9,5},{13,9},{6,2},{10,6},{14,10},{7,3},{... | collective-permute-start | bytes 15368 | tf_op jit(solution)/shard_map/ppermute | solution.py:28
  62.3 1.3 copy-start.6
  69.6 3.6 %copy-start.5 = (f32[512,512]{1,0:T(8,128)S(1)}, f32[512,512]{1,0:T(8,128)}, u32[]{:S(2)}) copy-start(f32[512,512]{1,0:T(8,128)} %get-tuple-element.25) | copy-start | bytes 3145732
  77.4 208.1 %all-reduce.7.cloned.1.call-start = ((), (), s32[]{:S(2)}) async-start(), calls=%async_computation.1 | async-start | bytes 6815744 | tf_op jit(solution)/shard_map/psum | solution.py:163
Sparse Core Ops, SparseCore 0:
  77.5 75.3 all-reduce.4
  155.3 130.1 all-reduce.6
